TPU v7x, 32 devices: a whole 2x2x4 slice. The times are simulated.
32 devices in a mesh: band: 2 (over y), col: 8 (over z, x), disp: 2 (over core).
Axes of the slice: x: 2, y: 2, z: 4, core: 2. Of those that a mesh axis runs over, the one named last changes fastest.
Arguments:
- left_feat: bfloat16 [8, 32, 2048], P('band', None, 'col'), parts along dimension 0, may hold values from -6 to 6
- right_feat: bfloat16 [8, 32, 2048], P('band', None, 'col'), parts along dimension 0, may hold values from -6 to 6
- w_first: bfloat16 [3, 3, 3, 32, 64], replicated, may hold values from -0.15625 to 0.15625
- w_second: bfloat16 [3, 3, 3, 1, 32], replicated, may hold values from -0.625 to 0.625
Outputs:
- disparity: float32 [8, 2048], P('band', 'col'), parts along dimension 0
- confidence: float32 [8, 2048], P('band', 'col'), parts along dimension 0
There are 2 independent parts, one for each index of `band`. A program takes and returns all parts, laid end to end along the dimension named above; an argument that names none is the same for every part. Nothing has to cross between parts.
All inputs are finite; a program needn't handle non-finite values.
Results may differ from a plain program's by a relative error of at most 0.0017.
Values may be sent and summed in bfloat16 or wider, within the bound.
A program may use at most 128 MiB of HBM per device.

v0:
```python
import functools

import jax
import jax.numpy as jnp
from jax import lax
from jax.experimental import pallas as pl
from jax.experimental.pallas import tpu as pltpu
from jax.sharding import PartitionSpec as P

DISP = 48
NEG = -1e30
NT = (((1,), (1,)), ((), ()))
MESH = pl.DeviceIdType.MESH


def banded(block, lane):
    return [
        jnp.where(lane < 64, pltpu.roll(block, 96, 1), 0.0),
        block,
        pltpu.roll(block, 32, 1),
        jnp.where(lane >= 64, pltpu.roll(block, 64, 1), 0.0),
    ]


def tables_kernel(n, left_hbm, right_hbm, w1_hbm, w2_hbm,
                  left_out, right_out, lfull, rfull, rtail, ends, w2b, halo_out,
                  lt, rt, wb, tl, tr, te, w1_ref, w2_ref, load_sem, send_sem, recv_sem):
    rows, feat, width = left_out.shape
    flat = rows * feat
    f32, bf16 = jnp.float32, jnp.bfloat16
    col = lax.axis_index("col")
    has_left = col > 0
    has_right = col < n - 1
    left_id = {"col": jnp.maximum(col - 1, 0)}
    right_id = {"col": jnp.minimum(col + 1, n - 1)}
    first = col == 0
    last = col == n - 1

    barrier = pltpu.get_barrier_semaphore()

    @pl.when(has_left)
    def _():
        pl.semaphore_signal(barrier, inc=1, device_id=left_id, device_id_type=MESH)

    @pl.when(has_right)
    def _():
        pl.semaphore_signal(barrier, inc=1, device_id=right_id, device_id_type=MESH)

    loads = [
        pltpu.make_async_copy(src, dst, load_sem.at[i])
        for i, (src, dst) in enumerate(
            ((right_hbm, right_out), (left_hbm, left_out), (w1_hbm, w1_ref), (w2_hbm, w2_ref)))
    ]
    for c in loads:
        c.start()

    rt[64 + width:72 + width, :] = jnp.zeros((8, flat), f32)

    @pl.when(first)
    def _():
        rt[0:56, :] = jnp.zeros((56, flat), f32)
        lt[0:8, :] = jnp.zeros((8, flat), f32)

    @pl.when(last)
    def _():
        rt[56 + width:64 + width, :] = jnp.zeros((8, flat), f32)
        lt[8 + width:16 + width, :] = jnp.zeros((8, flat), f32)

    w2b[...] = jnp.zeros_like(w2b)

    loads[0].wait()
    rt[56:56 + width, :] = right_out[...].reshape(flat, width).astype(f32).T
    loads[1].wait()
    lt[8:8 + width, :] = left_out[...].reshape(flat, width).astype(f32).T

    def copy(index, ref, src, dst, size, target):
        return pltpu.make_async_remote_copy(
            src_ref=ref.at[pl.ds(src, size)], dst_ref=ref.at[pl.ds(dst, size)],
            send_sem=send_sem.at[index], recv_sem=recv_sem.at[index],
            device_id=target, device_id_type=MESH)

    to_right = [copy(0, rt, width, 0, 56, right_id), copy(1, lt, width, 0, 8, right_id)]
    to_left = [copy(2, rt, 56, 56 + width, 8, left_id), copy(3, lt, 8, 8 + width, 8, left_id)]

    pl.semaphore_wait(barrier, has_left.astype(jnp.int32) + has_right.astype(jnp.int32))

    @pl.when(has_right)
    def _():
        for c in to_right:
            c.start()

    @pl.when(has_left)
    def _():
        for c in to_left:
            c.start()

    loads[2].wait()
    lane = lax.broadcasted_iota(jnp.int32, (32, 128), 1)
    zero = jnp.zeros((32, 32), f32)
    for a in range(3):
        for e in range(3):
            taps = [w1_ref[a, b, e].astype(f32) for b in range(3)]
            for side in range(2):
                block = jnp.concatenate([t[:, 32 * side:32 * side + 32] for t in taps] + [zero], axis=1)
                for ro, piece in enumerate(banded(block, lane)):
                    at = a * 128 + ro * 32
                    wb[side, at:at + 32, e * 128:(e + 1) * 128] = piece.astype(bf16)

    def taps_of(ref, start, count, side, used):
        lhs = jnp.concatenate(
            [ref[start + e:start + e + count, :].astype(bf16) for e in range(used)], axis=1)
        return lax.dot_general(lhs, wb[side, :, 0:128 * used], NT, preferred_element_type=f32)

    def fill(out, ref, at, count, side):
        res = taps_of(ref, at + 6, count, side, 3)
        for a in range(3):
            out[a, at:at + count, :] = res[:, a * 128:(a + 1) * 128]

    fill(tl, lt, 8, width - 8, 0)
    fill(tr, rt, 56, width - 8, 1)

    loads[3].wait()
    lane8 = lax.broadcasted_iota(jnp.int32, (8, 128), 1)
    for a in range(3):
        for e in range(3):
            taps = [w2_ref[a, b, e:e + 1, :].astype(f32) for b in range(3)]
            block = jnp.concatenate(taps + [jnp.zeros((1, 32), f32)], axis=1)
            pieces = banded(jnp.broadcast_to(block, (8, 128)), lane8)
            for di in range(2):
                do = di - (a - 1) + 1
                for ro in range(4):
                    at = e * 16 + do * 4 + ro
                    w2b[at:at + 1, di * 128:(di + 1) * 128] = pieces[ro][0:1, :]

    @pl.when(has_left)
    def _():
        for c in to_right:
            c.wait_recv()

    @pl.when(has_right)
    def _():
        for c in to_left:
            c.wait_recv()

    fill(tl, lt, 0, 8, 0)
    fill(tl, lt, width, 8, 0)
    fill(tr, rt, 0, 56, 1)
    fill(tr, rt, width + 48, 16, 1)
    res = taps_of(rt, width + 6, 64, 1, 2)
    for a in range(3):
        te[a, :, :] = res[:, a * 128:(a + 1) * 128]
    halo_out[...] = jnp.concatenate([jnp.zeros((8, 128), f32), rt[0:56, :]], axis=0).T.astype(bf16)

    line = lax.broadcasted_iota(jnp.int32, (width + 8, 128), 0)
    dead = (first & (line == 0)) | (last & (line >= width + 1))
    l_lo = tl[0, :, :]
    l_mid = tl[1, :, :]
    l_hi = tl[2, :, :]
    lfull[0:width + 8, :] = jnp.where(dead, NEG, l_lo + l_mid + l_hi)
    lfull[width + 8:width + 16, :] = jnp.full((8, 128), NEG, f32)
    rfull[...] = tr[0, 2:width + 58, :] + tr[1, 1:width + 57, :] + tr[2, 0:width + 56, :]
    edge = te[0, 2:58, :] + te[1, 1:57, :] + te[2, 0:56, :]
    rtail[0:56, :] = jnp.where(last, edge, rfull[width:width + 56, :])
    rtail[56:64, :] = jnp.zeros((8, 128), f32)

    for k, (value, a, s) in enumerate(((l_mid + l_hi, 1, DISP - 1), (l_lo + l_mid, 0, 1))):
        value = jnp.where(dead, NEG, value)
        body = tr[a, s + 1:s + 1 + width, :] + tr[a + 1, s:s + width, :]
        inner = tr[a, s + 1 + width:s + 9 + width, :] + tr[a + 1, s + width:s + 8 + width, :]
        outer = te[a, s + 1:s + 9, :] + te[a + 1, s:s + 8, :]
        tail = jnp.where(last, outer, inner)
        body = jnp.maximum(value[0:width] + body, 0.0)
        tail = jnp.maximum(value[width:width + 8] + tail, 0.0)
        ends[k, 0:width, :] = body.astype(bf16)
        ends[k, width:width + 16, :] = jnp.concatenate([tail, jnp.zeros((8, 128), f32)], axis=0).astype(bf16)

    @pl.when(has_right)
    def _():
        for c in to_right:
            c.wait_send()

    @pl.when(has_left)
    def _():
        for c in to_left:
            c.wait_send()


def cost_kernel(left_ref, right_ref, lfull, rfull, rtail, ends, w2b, halo_ref,
                disp_hbm, conf_hbm, disp_ref, conf_ref, sem):
    rows, feat, width = left_ref.shape
    flat = rows * feat
    f32, bf16 = jnp.float32, jnp.bfloat16

    def hidden(d):
        if d == 0:
            return ends[0]
        if d == DISP - 1:
            return ends[1]
        s = DISP - 1 - d
        body = jnp.maximum(lfull[0:width, :] + rfull[s:s + width, :], 0.0).astype(bf16)
        tail = jnp.maximum(lfull[width:width + 16, :] + rtail[s:s + 16, :], 0.0).astype(bf16)
        return jnp.concatenate([body, tail], axis=0)

    w2 = w2b[...].astype(jnp.bfloat16)
    low = lax.broadcasted_iota(jnp.int32, (8, width), 0) < 4
    total = jnp.zeros((8, width), jnp.float32)
    moment = jnp.zeros((8, width), jnp.float32)
    carry = None
    pairs = DISP // 2
    for k in range(pairs + 1):
        if k < pairs:
            both = jnp.concatenate([hidden(2 * k), hidden(2 * k + 1)], axis=1)
            q = lax.dot_general(w2, both, NT, preferred_element_type=jnp.float32)
            lows = [q[16 * e:16 * e + 8, :] for e in range(3)]
            highs = [q[16 * e + 8:16 * e + 16, :] for e in range(3)]
        if k == 0:
            sums = lows
        elif k == pairs:
            sums = carry
        else:
            sums = [x + y for x, y in zip(lows, carry)]
        carry = highs
        cost = sums[0][:, 0:width] + sums[1][:, 1:width + 1] + sums[2][:, 2:width + 2]
        expo = jnp.exp(-cost)
        if k == 0:
            expo = jnp.where(low, 0.0, expo)
        elif k == pairs:
            expo = jnp.where(low, expo, 0.0)
        total = total + expo
        moment = moment + expo * float(2 * k - 1)
    soft = (moment[0:4, :] + moment[4:8, :] + total[4:8, :]) / (total[0:4, :] + total[4:8, :])
    disp_ref[...] = soft / DISP
    save_disp = pltpu.make_async_copy(disp_ref, disp_hbm, sem.at[0])
    save_disp.start()

    held = jnp.minimum(soft, float(DISP - 1))
    halo = halo_ref[...]
    left_nat = left_ref[...].reshape(flat, width)
    right_nat = right_ref[...].reshape(flat, width)
    half = 128
    gap = (lax.broadcasted_iota(jnp.int32, (192, half), 1) - lax.broadcasted_iota(jnp.int32, (192, half), 0) + 64).astype(jnp.float32)
    for r in range(rows):
        band = slice(feat * r, feat * (r + 1))
        for h in range(width // half):
            want = held[r:r + 1, h * half:(h + 1) * half]
            weight = jnp.maximum(0.0, 1.0 - jnp.abs(want - gap))
            head = weight.astype(jnp.bfloat16)
            rest = (weight - head.astype(jnp.float32)).astype(jnp.bfloat16)
            own = right_nat[band, h * half:(h + 1) * half]
            if h == 0:
                before = halo[band, :]
            else:
                before = right_nat[band, (h - 1) * half + 64:h * half]
            warped = jnp.zeros((feat, half), jnp.float32)
            for part in (head, rest):
                warped = warped + jnp.dot(before, part[0:64, :], preferred_element_type=jnp.float32)
                warped = warped + jnp.dot(own, part[64:192, :], preferred_element_type=jnp.float32)
            off = jnp.abs(left_nat[band, h * half:(h + 1) * half].astype(jnp.float32) - warped)
            error = jnp.sum(off, axis=0, keepdims=True) * (1.0 / feat)
            conf_ref[r:r + 1, h * half:(h + 1) * half] = jnp.exp(-error)
    save_conf = pltpu.make_async_copy(conf_ref, conf_hbm, sem.at[1])
    save_conf.start()
    save_disp.wait()
    save_conf.wait()


def on_device(left_feat, right_feat, w_first, w_second):
    rows, feat, width = left_feat.shape
    n = lax.axis_size("col")
    f32, bf16 = jnp.float32, jnp.bfloat16
    w_cost = w_second[:, :, :, 0, :]
    vmem = pl.BlockSpec(memory_space=pltpu.VMEM)
    hbm = pl.BlockSpec(memory_space=pltpu.HBM)
    shape = jax.ShapeDtypeStruct
    tables = pl.pallas_call(
        functools.partial(tables_kernel, n),
        out_shape=(
            shape(left_feat.shape, bf16),
            shape(right_feat.shape, bf16),
            shape((width + 16, 128), f32),
            shape((width + 56, 128), f32),
            shape((64, 128), f32),
            shape((2, width + 16, 128), bf16),
            shape((48, 256), f32),
            shape((128, 64), bf16),
        ),
        in_specs=[hbm] * 4,
        out_specs=(vmem,) * 8,
        scratch_shapes=[
            pltpu.VMEM((width + 16, 128), f32),
            pltpu.VMEM((width + 72, 128), f32),
            pltpu.VMEM((2, 384, 384), bf16),
            pltpu.VMEM((3, width + 8, 128), f32),
            pltpu.VMEM((3, width + 64, 128), f32),
            pltpu.VMEM((3, 64, 128), f32),
            pltpu.VMEM(w_first.shape, bf16),
            pltpu.VMEM(w_cost.shape, bf16),
            pltpu.SemaphoreType.DMA((4,)),
            pltpu.SemaphoreType.DMA((4,)),
            pltpu.SemaphoreType.DMA((4,)),
        ],
        compiler_params=pltpu.CompilerParams(
            collective_id=0, has_side_effects=True, vmem_limit_bytes=16 << 20),
    )(*(pltpu.with_memory_space_constraint(x, pltpu.HBM) for x in (left_feat, right_feat, w_first, w_cost)))
    out = shape((rows, width), f32)
    return pl.pallas_call(
        cost_kernel,
        out_shape=(out, out),
        in_specs=[vmem] * 8,
        out_specs=(hbm, hbm),
        scratch_shapes=[
            pltpu.VMEM((rows, width), f32),
            pltpu.VMEM((rows, width), f32),
            pltpu.SemaphoreType.DMA((2,)),
        ],
        compiler_params=pltpu.CompilerParams(vmem_limit_bytes=16 << 20),
    )(*tables)


def solution(mesh):
    in_specs = (P("band", None, "col"), P("band", None, "col"), P(), P())
    out_specs = (P("band", "col"), P("band", "col"))
    return jax.shard_map(
        on_device, mesh=mesh, in_specs=in_specs, out_specs=out_specs, check_vma=False
    )
```

profile of v0, /device:TPU:0, one launch (start us, length us, event | category | flops | bytes accessed | tf_op | source)
XLA Modules:
  0.0 9.8 jit_solution(5138717986674308257)
XLA Ops:
  0.6 6.9 %shard_map.59 = (bf16[4,32,256]{2,1,0:T(8,128)(2,1)S(1)}, bf16[4,32,256]{2,1,0:T(8,128)(2,1)S(1)}, f32[272,128]{1,0:T(8,128)S(1)}, f32[312,128]{1,0:T(8,128)S(1)...) custom-call(bf16[4,32,256]{2,1,0:T(8,128)(2,1)} %left_hbm.1, ...), custom_call_target="tpu_custom_call" | custom-call | tf_op jit(solution)/shard_map/pallas_call | solution.py:275
  7.5 2.3 %shard_map.60 = (f32[4,256]{1,0:T(4,128)}, f32[4,256]{1,0:T(4,128)}) custom-call(bf16[4,32,256]{2,1,0:T(8,128)(2,1)S(1)} %get-tuple-element.10.left_ref, bf16[4,32,256]{2,1,0:T(8,128)(2,1)S(1)} %get-tuple-element.11.right_ref, f32[272,128]{1,0:T(8,128)S(1)} %get-tuple-element.12.lfull, f32[312,128]{1,0:T(8,128)S(1)} %get-tuple-element.13.rfull, ...), custom_call_target="tpu_custom_call" | custom-call | tf_op jit(solution)/shard_map/pallas_call | solution.py:306
where the time goes:
time: 9.97 us; the launch traced here: 9.82 us
  Pallas kernels  9.18 us (92%)
  between operations  0.64 us (6%)
    pallas_call x1, Pallas kernels, on_device(): pl.pallas_call(functools.partial(tables_kernel, n), out_shape=(shape(left...  6.89 us
    pallas_call x1, Pallas kernels, on_device(): pl.pallas_call(cost_kernel, out_shape=(out, out), in_specs=[vmem] * 8, ou...  2.29 us

commit v1 on v0

--- a/solution.py
+++ b/solution.py
@@ -24,7 +24,7 @@
 
 def tables_kernel(n, left_hbm, right_hbm, w1_hbm, w2_hbm,
                   left_out, right_out, lfull, rfull, rtail, ends, w2b, halo_out,
-                  lt, rt, wb, tl, tr, te, w1_ref, w2_ref, load_sem, send_sem, recv_sem):
+                  lt, rt, wb, tl, tr, te, w1_ref, w2_ref, out_r, out_l, in_l, in_r, load_sem, send_sem, recv_sem):
     rows, feat, width = left_out.shape
     flat = rows * feat
     f32, bf16 = jnp.float32, jnp.bfloat16
@@ -73,26 +73,28 @@
     loads[1].wait()
     lt[8:8 + width, :] = left_out[...].reshape(flat, width).astype(f32).T
 
-    def copy(index, ref, src, dst, size, target):
+    out_r[0:64, :] = rt[width - 8:width + 56, :].astype(bf16)
+    out_r[64:80, :] = lt[width - 8:width + 8, :].astype(bf16)
+    out_l[0:16, :] = rt[56:72, :].astype(bf16)
+    out_l[16:32, :] = lt[8:24, :].astype(bf16)
+
+    def copy(index, src, dst, target):
         return pltpu.make_async_remote_copy(
-            src_ref=ref.at[pl.ds(src, size)], dst_ref=ref.at[pl.ds(dst, size)],
-            send_sem=send_sem.at[index], recv_sem=recv_sem.at[index],
+            src_ref=src, dst_ref=dst, send_sem=send_sem.at[index], recv_sem=recv_sem.at[index],
             device_id=target, device_id_type=MESH)
 
-    to_right = [copy(0, rt, width, 0, 56, right_id), copy(1, lt, width, 0, 8, right_id)]
-    to_left = [copy(2, rt, 56, 56 + width, 8, left_id), copy(3, lt, 8, 8 + width, 8, left_id)]
+    to_right = copy(0, out_r, in_l, right_id)
+    to_left = copy(1, out_l, in_r, left_id)
 
     pl.semaphore_wait(barrier, has_left.astype(jnp.int32) + has_right.astype(jnp.int32))
 
     @pl.when(has_right)
     def _():
-        for c in to_right:
-            c.start()
+        to_right.start()
 
     @pl.when(has_left)
     def _():
-        for c in to_left:
-            c.start()
+        to_left.start()
 
     loads[2].wait()
     lane = lax.broadcasted_iota(jnp.int32, (32, 128), 1)
@@ -106,18 +108,42 @@
                     at = a * 128 + ro * 32
                     wb[side, at:at + 32, e * 128:(e + 1) * 128] = piece.astype(bf16)
 
-    def taps_of(ref, start, count, side, used):
-        lhs = jnp.concatenate(
-            [ref[start + e:start + e + count, :].astype(bf16) for e in range(used)], axis=1)
-        return lax.dot_general(lhs, wb[side, :, 0:128 * used], NT, preferred_element_type=f32)
-
-    def fill(out, ref, at, count, side):
-        res = taps_of(ref, at + 6, count, side, 3)
-        for a in range(3):
-            out[a, at:at + count, :] = res[:, a * 128:(a + 1) * 128]
-
-    fill(tl, lt, 8, width - 8, 0)
-    fill(tr, rt, 56, width - 8, 1)
+    def shifted(ref, start, count, used=3):
+        parts = [ref[start + e:start + e + count, :].astype(bf16) for e in range(used)]
+        return jnp.concatenate(parts + [jnp.zeros((count, 128), bf16)] * (3 - used), axis=1)
+
+    def fill(side, pieces):
+        lhs = [shifted(ref, start, count, used) for ref, start, count, used, _, _ in pieces]
+        lhs = lhs[0] if len(lhs) == 1 else jnp.concatenate(lhs, axis=0)
+        res = lax.dot_general(lhs, wb[side], NT, preferred_element_type=f32)
+        at = 0
+        for _, _, count, _, out, to in pieces:
+            for a in range(3):
+                out[a, to:to + count, :] = res[at:at + count, a * 128:(a + 1) * 128]
+            at += count
+
+    def left_table(taps, lo, hi):
+        value = sum(tl[a, lo:hi, :] for a in taps)
+        line = lo + lax.broadcasted_iota(jnp.int32, (hi - lo, 128), 0)
+        dead = (first & (line == 0)) | (last & (line >= width + 1))
+        return jnp.where(dead, NEG, value)
+
+    def right_table(lo, hi):
+        rfull[lo:hi, :] = tr[0, lo + 2:hi + 2, :] + tr[1, lo + 1:hi + 1, :] + tr[2, lo:hi, :]
+
+    end_taps = ((1, 2, DISP - 1), (0, 1, 1))
+
+    def end_rows(k, lo, hi):
+        a, b, s = end_taps[k]
+        body = tr[a, s + 1 + lo:s + 1 + hi, :] + tr[b, s + lo:s + hi, :]
+        ends[k, lo:hi, :] = jnp.maximum(left_table((a, b), lo, hi) + body, 0.0).astype(bf16)
+
+    fill(0, [(lt, 14, width - 8, 3, tl, 8)])
+    fill(1, [(rt, 62, width - 8, 3, tr, 56)])
+    lfull[8:width, :] = left_table((0, 1, 2), 8, width)
+    right_table(56, width + 40)
+    end_rows(0, 16, width - 16)
+    end_rows(1, 64, width - 16)
 
     loads[3].wait()
     lane8 = lax.broadcasted_iota(jnp.int32, (8, 128), 1)
@@ -134,55 +160,45 @@
 
     @pl.when(has_left)
     def _():
-        for c in to_right:
-            c.wait_recv()
+        to_right.wait_recv()
+        rt[0:56, :] = in_l[8:64, :].astype(f32)
+        lt[0:8, :] = in_l[72:80, :].astype(f32)
 
     @pl.when(has_right)
     def _():
-        for c in to_left:
-            c.wait_recv()
-
-    fill(tl, lt, 0, 8, 0)
-    fill(tl, lt, width, 8, 0)
-    fill(tr, rt, 0, 56, 1)
-    fill(tr, rt, width + 48, 16, 1)
-    res = taps_of(rt, width + 6, 64, 1, 2)
-    for a in range(3):
-        te[a, :, :] = res[:, a * 128:(a + 1) * 128]
+        to_left.wait_recv()
+        rt[56 + width:64 + width, :] = in_r[0:8, :].astype(f32)
+        lt[8 + width:16 + width, :] = in_r[16:24, :].astype(f32)
+
+    fill(1, [(rt, 6, 56, 3, tr, 0), (rt, width + 54, 16, 3, tr, width + 48), (rt, width + 6, 64, 2, te, 0)])
+    fill(0, [(lt, 6, 8, 3, tl, 0), (lt, width + 6, 8, 3, tl, width)])
     halo_out[...] = jnp.concatenate([jnp.zeros((8, 128), f32), rt[0:56, :]], axis=0).T.astype(bf16)
 
-    line = lax.broadcasted_iota(jnp.int32, (width + 8, 128), 0)
-    dead = (first & (line == 0)) | (last & (line >= width + 1))
-    l_lo = tl[0, :, :]
-    l_mid = tl[1, :, :]
-    l_hi = tl[2, :, :]
-    lfull[0:width + 8, :] = jnp.where(dead, NEG, l_lo + l_mid + l_hi)
+    lfull[0:8, :] = left_table((0, 1, 2), 0, 8)
+    lfull[width:width + 8, :] = left_table((0, 1, 2), width, width + 8)
     lfull[width + 8:width + 16, :] = jnp.full((8, 128), NEG, f32)
-    rfull[...] = tr[0, 2:width + 58, :] + tr[1, 1:width + 57, :] + tr[2, 0:width + 56, :]
+    right_table(0, 56)
+    right_table(width + 40, width + 56)
     edge = te[0, 2:58, :] + te[1, 1:57, :] + te[2, 0:56, :]
     rtail[0:56, :] = jnp.where(last, edge, rfull[width:width + 56, :])
     rtail[56:64, :] = jnp.zeros((8, 128), f32)
-
-    for k, (value, a, s) in enumerate(((l_mid + l_hi, 1, DISP - 1), (l_lo + l_mid, 0, 1))):
-        value = jnp.where(dead, NEG, value)
-        body = tr[a, s + 1:s + 1 + width, :] + tr[a + 1, s:s + width, :]
-        inner = tr[a, s + 1 + width:s + 9 + width, :] + tr[a + 1, s + width:s + 8 + width, :]
-        outer = te[a, s + 1:s + 9, :] + te[a + 1, s:s + 8, :]
-        tail = jnp.where(last, outer, inner)
-        body = jnp.maximum(value[0:width] + body, 0.0)
-        tail = jnp.maximum(value[width:width + 8] + tail, 0.0)
-        ends[k, 0:width, :] = body.astype(bf16)
+    end_rows(0, 0, 16)
+    end_rows(0, width - 16, width)
+    end_rows(1, 0, 64)
+    end_rows(1, width - 16, width)
+    for k, (a, b, s) in enumerate(end_taps):
+        inner = tr[a, s + 1 + width:s + 9 + width, :] + tr[b, s + width:s + 8 + width, :]
+        outer = te[a, s + 1:s + 9, :] + te[b, s:s + 8, :]
+        tail = jnp.maximum(left_table((a, b), width, width + 8) + jnp.where(last, outer, inner), 0.0)
         ends[k, width:width + 16, :] = jnp.concatenate([tail, jnp.zeros((8, 128), f32)], axis=0).astype(bf16)
 
     @pl.when(has_right)
     def _():
-        for c in to_right:
-            c.wait_send()
+        to_right.wait_send()
 
     @pl.when(has_left)
     def _():
-        for c in to_left:
-            c.wait_send()
+        to_left.wait_send()
 
 
 def cost_kernel(left_ref, right_ref, lfull, rfull, rtail, ends, w2b, halo_ref,
@@ -295,9 +311,13 @@
             pltpu.VMEM((3, 64, 128), f32),
             pltpu.VMEM(w_first.shape, bf16),
             pltpu.VMEM(w_cost.shape, bf16),
+            pltpu.VMEM((80, 128), bf16),
+            pltpu.VMEM((32, 128), bf16),
+            pltpu.VMEM((80, 128), bf16),
+            pltpu.VMEM((32, 128), bf16),
             pltpu.SemaphoreType.DMA((4,)),
-            pltpu.SemaphoreType.DMA((4,)),
-            pltpu.SemaphoreType.DMA((4,)),
+            pltpu.SemaphoreType.DMA((2,)),
+            pltpu.SemaphoreType.DMA((2,)),
         ],
         compiler_params=pltpu.CompilerParams(
             collective_id=0, has_side_effects=True, vmem_limit_bytes=16 << 20),

time: 9.97 us -> 9.62 us (0.965)
  Pallas kernels: 9.18 us -> 8.83 us
    pallas_call x1, Pallas kernels: 6.89 us -> 6.54 us  [on_device(): pl.pallas_call(functools.partial(tables_kernel, n), out_shape=(shape(left...]
where the time goes in v1:
time: 9.62 us; the launch traced here: 9.47 us
  Pallas kernels  8.83 us (92%)
  between operations  0.64 us (7%)
    pallas_call x1, Pallas kernels, on_device(): pl.pallas_call(functools.partial(tables_kernel, n), out_shape=(shape(left...  6.54 us
    pallas_call x1, Pallas kernels, on_device(): pl.pallas_call(cost_kernel, out_shape=(out, out), in_specs=[vmem] * 8, ou...  2.29 us

profile of v1, /device:TPU:0, one launch (start us, length us, event | category | flops | bytes accessed | tf_op | source)
XLA Modules:
  0.0 9.5 jit_solution(4321526813927761541)
XLA Ops:
  0.6 6.5 %shard_map.59 = (bf16[4,32,256]{2,1,0:T(8,128)(2,1)S(1)}, bf16[4,32,256]{2,1,0:T(8,128)(2,1)S(1)}, f32[272,128]{1,0:T(8,128)S(1)}, f32[312,128]{1,0:T(8,128)S(1)...) custom-call(bf16[4,32,256]{2,1,0:T(8,128)(2,1)} %left_hbm.1, ...), custom_call_target="tpu_custom_call" | custom-call | tf_op jit(solution)/shard_map/pallas_call | solution.py:291
  7.2 2.3 %shard_map.60 = (f32[4,256]{1,0:T(4,128)}, f32[4,256]{1,0:T(4,128)}) custom-call(bf16[4,32,256]{2,1,0:T(8,128)(2,1)S(1)} %get-tuple-element.10.left_ref, bf16[4,32,256]{2,1,0:T(8,128)(2,1)S(1)} %get-tuple-element.11.right_ref, f32[272,128]{1,0:T(8,128)S(1)} %get-tuple-element.12.lfull, f32[312,128]{1,0:T(8,128)S(1)} %get-tuple-element.13.rfull, ...), custom_call_target="tpu_custom_call" | custom-call | tf_op jit(solution)/shard_map/pallas_call | solution.py:326

commit v2 on v1

--- a/solution.py
+++ b/solution.py
@@ -22,8 +22,27 @@
     ]
 
 
+def cost_sums(weights, hidden):
+    carry = None
+    pairs = DISP // 2
+    for k in range(pairs + 1):
+        if k < pairs:
+            both = jnp.concatenate([hidden(2 * k), hidden(2 * k + 1)], axis=1)
+            q = lax.dot_general(weights, both, NT, preferred_element_type=jnp.float32)
+            lows = [q[16 * e:16 * e + 8, :] for e in range(3)]
+            highs = [q[16 * e + 8:16 * e + 16, :] for e in range(3)]
+        if k == 0:
+            sums = lows
+        elif k == pairs:
+            sums = carry
+        else:
+            sums = [x + y for x, y in zip(lows, carry)]
+        carry = highs
+        yield k, sums
+
+
 def tables_kernel(n, left_hbm, right_hbm, w1_hbm, w2_hbm,
-                  left_out, right_out, lfull, rfull, rtail, ends, w2b, halo_out,
+                  left_out, right_out, lfull, rfull, rtail, ends, w2b, halo_out, costs,
                   lt, rt, wb, tl, tr, te, w1_ref, w2_ref, out_r, out_l, in_l, in_r, load_sem, send_sem, recv_sem):
     rows, feat, width = left_out.shape
     flat = rows * feat
@@ -137,13 +156,6 @@
         a, b, s = end_taps[k]
         body = tr[a, s + 1 + lo:s + 1 + hi, :] + tr[b, s + lo:s + hi, :]
         ends[k, lo:hi, :] = jnp.maximum(left_table((a, b), lo, hi) + body, 0.0).astype(bf16)
-
-    fill(0, [(lt, 14, width - 8, 3, tl, 8)])
-    fill(1, [(rt, 62, width - 8, 3, tr, 56)])
-    lfull[8:width, :] = left_table((0, 1, 2), 8, width)
-    right_table(56, width + 40)
-    end_rows(0, 16, width - 16)
-    end_rows(1, 64, width - 16)
 
     loads[3].wait()
     lane8 = lax.broadcasted_iota(jnp.int32, (8, 128), 1)
@@ -158,6 +170,27 @@
                     at = e * 16 + do * 4 + ro
                     w2b[at:at + 1, di * 128:(di + 1) * 128] = pieces[ro][0:1, :]
 
+    fill(0, [(lt, 14, width - 8, 3, tl, 8)])
+    fill(1, [(rt, 62, width - 8, 3, tr, 56)])
+    lfull[8:width, :] = left_table((0, 1, 2), 8, width)
+    right_table(56, width + 46)
+    end_rows(0, 16, width)
+    end_rows(1, 64, width)
+
+    half = width // 2
+
+    def hidden(d):
+        if d == 0:
+            return ends[0, half:width, :]
+        if d == DISP - 1:
+            return ends[1, half:width, :]
+        s = DISP - 1 - d
+        return jnp.maximum(lfull[half:width, :] + rfull[s + half:s + width, :], 0.0).astype(bf16)
+
+    for k, (one, two, three) in cost_sums(w2b[...].astype(bf16), hidden):
+        costs[k] = one + pltpu.roll(two, half - 1, 1) + pltpu.roll(three, half - 2, 1)
+
+
     @pl.when(has_left)
     def _():
         to_right.wait_recv()
@@ -183,9 +216,7 @@
     rtail[0:56, :] = jnp.where(last, edge, rfull[width:width + 56, :])
     rtail[56:64, :] = jnp.zeros((8, 128), f32)
     end_rows(0, 0, 16)
-    end_rows(0, width - 16, width)
     end_rows(1, 0, 64)
-    end_rows(1, width - 16, width)
     for k, (a, b, s) in enumerate(end_taps):
         inner = tr[a, s + 1 + width:s + 9 + width, :] + tr[b, s + width:s + 8 + width, :]
         outer = te[a, s + 1:s + 9, :] + te[b, s:s + 8, :]
@@ -201,42 +232,37 @@
         to_left.wait_send()
 
 
-def cost_kernel(left_ref, right_ref, lfull, rfull, rtail, ends, w2b, halo_ref,
+def cost_kernel(left_ref, right_ref, lfull, rfull, rtail, ends, w2b, halo_ref, costs,
                 disp_hbm, conf_hbm, disp_ref, conf_ref, sem):
     rows, feat, width = left_ref.shape
     flat = rows * feat
     f32, bf16 = jnp.float32, jnp.bfloat16
 
+    half = width // 2
+    lo, hi = half + 8, width - 8
+
     def hidden(d):
-        if d == 0:
-            return ends[0]
-        if d == DISP - 1:
-            return ends[1]
+        if d == 0 or d == DISP - 1:
+            k = 0 if d == 0 else 1
+            parts = [ends[k, 0:lo, :].astype(f32), ends[k, hi:width + 16, :].astype(f32)]
+            return jnp.concatenate(parts, axis=0).astype(bf16)
         s = DISP - 1 - d
-        body = jnp.maximum(lfull[0:width, :] + rfull[s:s + width, :], 0.0).astype(bf16)
-        tail = jnp.maximum(lfull[width:width + 16, :] + rtail[s:s + 16, :], 0.0).astype(bf16)
-        return jnp.concatenate([body, tail], axis=0)
-
-    w2 = w2b[...].astype(jnp.bfloat16)
+        parts = [
+            lfull[0:lo, :] + rfull[s:s + lo, :],
+            lfull[hi:width, :] + rfull[s + hi:s + width, :],
+            lfull[width:width + 16, :] + rtail[s:s + 16, :],
+        ]
+        return jnp.maximum(jnp.concatenate(parts, axis=0), 0.0).astype(bf16)
+
     low = lax.broadcasted_iota(jnp.int32, (8, width), 0) < 4
+    ready = lax.broadcasted_iota(jnp.int32, (8, half), 1) < half - 2
     total = jnp.zeros((8, width), jnp.float32)
     moment = jnp.zeros((8, width), jnp.float32)
-    carry = None
     pairs = DISP // 2
-    for k in range(pairs + 1):
-        if k < pairs:
-            both = jnp.concatenate([hidden(2 * k), hidden(2 * k + 1)], axis=1)
-            q = lax.dot_general(w2, both, NT, preferred_element_type=jnp.float32)
-            lows = [q[16 * e:16 * e + 8, :] for e in range(3)]
-            highs = [q[16 * e + 8:16 * e + 16, :] for e in range(3)]
-        if k == 0:
-            sums = lows
-        elif k == pairs:
-            sums = carry
-        else:
-            sums = [x + y for x, y in zip(lows, carry)]
-        carry = highs
-        cost = sums[0][:, 0:width] + sums[1][:, 1:width + 1] + sums[2][:, 2:width + 2]
+    for k, sums in cost_sums(w2b[...].astype(bf16), hidden):
+        near = sums[0][:, 0:half] + sums[1][:, 1:half + 1] + sums[2][:, 2:half + 2]
+        edge = sums[0][:, 16:half + 16] + sums[1][:, 17:half + 17] + sums[2][:, 18:half + 18]
+        cost = jnp.concatenate([near, jnp.where(ready, costs[k], edge)], axis=1)
         expo = jnp.exp(-cost)
         if k == 0:
             expo = jnp.where(low, 0.0, expo)
@@ -253,7 +279,6 @@
     halo = halo_ref[...]
     left_nat = left_ref[...].reshape(flat, width)
     right_nat = right_ref[...].reshape(flat, width)
-    half = 128
     gap = (lax.broadcasted_iota(jnp.int32, (192, half), 1) - lax.broadcasted_iota(jnp.int32, (192, half), 0) + 64).astype(jnp.float32)
     for r in range(rows):
         band = slice(feat * r, feat * (r + 1))
@@ -299,9 +324,10 @@
             shape((2, width + 16, 128), bf16),
             shape((48, 256), f32),
             shape((128, 64), bf16),
+            shape((DISP // 2 + 1, 8, width // 2), f32),
         ),
         in_specs=[hbm] * 4,
-        out_specs=(vmem,) * 8,
+        out_specs=(vmem,) * 9,
         scratch_shapes=[
             pltpu.VMEM((width + 16, 128), f32),
             pltpu.VMEM((width + 72, 128), f32),
@@ -326,7 +352,7 @@
     return pl.pallas_call(
         cost_kernel,
         out_shape=(out, out),
-        in_specs=[vmem] * 8,
+        in_specs=[vmem] * 9,
         out_specs=(hbm, hbm),
         scratch_shapes=[
             pltpu.VMEM((rows, width), f32),

time: 9.62 us -> 9.24 us (0.960)
  Pallas kernels: 8.83 us -> 8.45 us
    pallas_call x1, Pallas kernels: 2.29 us -> 1.91 us  [on_device(): pl.pallas_call(cost_kernel, out_shape=(out, out), in_specs=[vmem] * 9, ou...]
where the time goes in v2:
time: 9.24 us; the launch traced here: 9.09 us
  Pallas kernels  8.45 us (91%)
  between operations  0.64 us (7%)
    pallas_call x1, Pallas kernels, on_device(): pl.pallas_call(functools.partial(tables_kernel, n), out_shape=(shape(left...  6.54 us
    pallas_call x1, Pallas kernels, on_device(): pl.pallas_call(cost_kernel, out_shape=(out, out), in_specs=[vmem] * 9, ou...  1.91 us

profile of v2, /device:TPU:0, one launch (start us, length us, event | category | flops | bytes accessed | tf_op | source)
XLA Modules:
  0.0 9.1 jit_solution(17443553962135334563)
XLA Ops:
  0.6 6.5 %shard_map.59 = (bf16[4,32,256]{2,1,0:T(8,128)(2,1)S(1)}, bf16[4,32,256]{2,1,0:T(8,128)(2,1)S(1)}, f32[272,128]{1,0:T(8,128)S(1)}, f32[312,128]{1,0:T(8,128)S(1)...) custom-call(bf16[4,32,256]{2,1,0:T(8,128)(2,1)} %left_hbm.1, ...), custom_call_target="tpu_custom_call" | custom-call | tf_op jit(solution)/shard_map/pallas_call | solution.py:316
  7.2 1.9 %shard_map.60 = (f32[4,256]{1,0:T(4,128)}, f32[4,256]{1,0:T(4,128)}) custom-call(bf16[4,32,256]{2,1,0:T(8,128)(2,1)S(1)} %get-tuple-element.11.left_ref, bf16[4,32,256]{2,1,0:T(8,128)(2,1)S(1)} %get-tuple-element.12.right_ref, f32[272,128]{1,0:T(8,128)S(1)} %get-tuple-element.13.lfull, f32[312,128]{1,0:T(8,128)S(1)} %get-tuple-element.14.rfull, ...), custom_call_target="tpu_custom_call" | custom-call | tf_op jit(solution)/shard_map/pallas_call | solution.py:352

commit v3 on v2

--- a/solution.py
+++ b/solution.py
@@ -87,16 +87,6 @@
 
     w2b[...] = jnp.zeros_like(w2b)
 
-    loads[0].wait()
-    rt[56:56 + width, :] = right_out[...].reshape(flat, width).astype(f32).T
-    loads[1].wait()
-    lt[8:8 + width, :] = left_out[...].reshape(flat, width).astype(f32).T
-
-    out_r[0:64, :] = rt[width - 8:width + 56, :].astype(bf16)
-    out_r[64:80, :] = lt[width - 8:width + 8, :].astype(bf16)
-    out_l[0:16, :] = rt[56:72, :].astype(bf16)
-    out_l[16:32, :] = lt[8:24, :].astype(bf16)
-
     def copy(index, src, dst, target):
         return pltpu.make_async_remote_copy(
             src_ref=src, dst_ref=dst, send_sem=send_sem.at[index], recv_sem=recv_sem.at[index],
@@ -105,15 +95,35 @@
     to_right = copy(0, out_r, in_l, right_id)
     to_left = copy(1, out_l, in_r, left_id)
 
+    def turned(ref, lo, hi):
+        return ref[:, :, lo:hi].reshape(flat, hi - lo).astype(f32).T
+
+    loads[0].wait()
+    r_tail = turned(right_out, width - 128, width)
+    out_r[0:64, :] = r_tail[64:128, :].astype(bf16)
+    loads[1].wait()
+    l_tail = turned(left_out, width - 128, width)
+    out_r[64:80, :] = l_tail[112:128, :].astype(bf16)
+
     pl.semaphore_wait(barrier, has_left.astype(jnp.int32) + has_right.astype(jnp.int32))
 
     @pl.when(has_right)
     def _():
         to_right.start()
 
+    r_head = turned(right_out, 0, width - 128)
+    l_head = turned(left_out, 0, width - 128)
+    out_l[0:16, :] = r_head[0:16, :].astype(bf16)
+    out_l[16:32, :] = l_head[0:16, :].astype(bf16)
+
     @pl.when(has_left)
     def _():
         to_left.start()
+
+    rt[56:width - 72, :] = r_head
+    rt[width - 72:width + 56, :] = r_tail
+    lt[8:width - 120, :] = l_head
+    lt[width - 120:width + 8, :] = l_tail
 
     loads[2].wait()
     lane = lax.broadcasted_iota(jnp.int32, (32, 128), 1)
@@ -205,7 +215,7 @@
 
     fill(1, [(rt, 6, 56, 3, tr, 0), (rt, width + 54, 16, 3, tr, width + 48), (rt, width + 6, 64, 2, te, 0)])
     fill(0, [(lt, 6, 8, 3, tl, 0), (lt, width + 6, 8, 3, tl, width)])
-    halo_out[...] = jnp.concatenate([jnp.zeros((8, 128), f32), rt[0:56, :]], axis=0).T.astype(bf16)
+    halo_out[...] = jnp.concatenate([jnp.zeros((72, 128), f32), rt[0:56, :]], axis=0).T.astype(bf16)
 
     lfull[0:8, :] = left_table((0, 1, 2), 0, 8)
     lfull[width:width + 8, :] = left_table((0, 1, 2), width, width + 8)
@@ -280,6 +290,7 @@
     left_nat = left_ref[...].reshape(flat, width)
     right_nat = right_ref[...].reshape(flat, width)
     gap = (lax.broadcasted_iota(jnp.int32, (192, half), 1) - lax.broadcasted_iota(jnp.int32, (192, half), 0) + 64).astype(jnp.float32)
+    blank = jnp.zeros((64, half), jnp.bfloat16)
     for r in range(rows):
         band = slice(feat * r, feat * (r + 1))
         for h in range(width // half):
@@ -287,15 +298,14 @@
             weight = jnp.maximum(0.0, 1.0 - jnp.abs(want - gap))
             head = weight.astype(jnp.bfloat16)
             rest = (weight - head.astype(jnp.float32)).astype(jnp.bfloat16)
-            own = right_nat[band, h * half:(h + 1) * half]
             if h == 0:
-                before = halo[band, :]
+                cols = jnp.concatenate([halo[band, :], right_nat[band, 0:half]], axis=1)
             else:
-                before = right_nat[band, (h - 1) * half + 64:h * half]
+                cols = right_nat[band, (h - 1) * half:(h + 1) * half]
             warped = jnp.zeros((feat, half), jnp.float32)
             for part in (head, rest):
-                warped = warped + jnp.dot(before, part[0:64, :], preferred_element_type=jnp.float32)
-                warped = warped + jnp.dot(own, part[64:192, :], preferred_element_type=jnp.float32)
+                part = jnp.concatenate([blank, part], axis=0)
+                warped = warped + jnp.dot(cols, part, preferred_element_type=jnp.float32)
             off = jnp.abs(left_nat[band, h * half:(h + 1) * half].astype(jnp.float32) - warped)
             error = jnp.sum(off, axis=0, keepdims=True) * (1.0 / feat)
             conf_ref[r:r + 1, h * half:(h + 1) * half] = jnp.exp(-error)
@@ -323,7 +333,7 @@
             shape((64, 128), f32),
             shape((2, width + 16, 128), bf16),
             shape((48, 256), f32),
-            shape((128, 64), bf16),
+            shape((128, 128), bf16),
             shape((DISP // 2 + 1, 8, width // 2), f32),
         ),
         in_specs=[hbm] * 4,

time: 9.24 us -> 9.27 us (level)
  no operation moved by 1% of the time
where the time goes in v3:
time: 9.27 us; the launch traced here: 9.11 us
  Pallas kernels  8.48 us (91%)
  between operations  0.64 us (7%)
    pallas_call x1, Pallas kernels, on_device(): pl.pallas_call(functools.partial(tables_kernel, n), out_shape=(shape(left...  6.61 us
    pallas_call x1, Pallas kernels, on_device(): pl.pallas_call(cost_kernel, out_shape=(out, out), in_specs=[vmem] * 9, ou...  1.86 us

profile of v3, /device:TPU:0, one launch (start us, length us, event | category | flops | bytes accessed | tf_op | source)
XLA Modules:
  0.0 9.1 jit_solution(8217523453664463603)
XLA Ops:
  0.6 6.6 %shard_map.59 = (bf16[4,32,256]{2,1,0:T(8,128)(2,1)S(1)}, bf16[4,32,256]{2,1,0:T(8,128)(2,1)S(1)}, f32[272,128]{1,0:T(8,128)S(1)}, f32[312,128]{1,0:T(8,128)S(1)...) custom-call(bf16[4,32,256]{2,1,0:T(8,128)(2,1)} %left_hbm.1, ...), custom_call_target="tpu_custom_call" | custom-call | tf_op jit(solution)/shard_map/pallas_call | solution.py:326
  7.3 1.9 %shard_map.60 = (f32[4,256]{1,0:T(4,128)}, f32[4,256]{1,0:T(4,128)}) custom-call(bf16[4,32,256]{2,1,0:T(8,128)(2,1)S(1)} %get-tuple-element.11.left_ref, bf16[4,32,256]{2,1,0:T(8,128)(2,1)S(1)} %get-tuple-element.12.right_ref, f32[272,128]{1,0:T(8,128)S(1)} %get-tuple-element.13.lfull, f32[312,128]{1,0:T(8,128)S(1)} %get-tuple-element.14.rfull, ...), custom_call_target="tpu_custom_call" | custom-call | tf_op jit(solution)/shard_map/pallas_call | solution.py:362
